TPU v7x, 32 devices: a whole 2x2x4 slice. The times are simulated.
32 devices in a mesh: dp: 16 (over z, x, core), tensor: 2 (over y).
Axes of the slice: x: 2, y: 2, z: 4, core: 2. Of those that a mesh axis runs over, the one named last changes fastest.
Arguments:
- hidden_in: bfloat16 [16384, 1024], P(('dp', 'tensor')), may hold values from -6 to 6
- positions: int32 [16384], P('dp'), may hold values from 0 to 1023, as said below
- gain_attention: float32 [1024], replicated, may hold values from 0.1 to 1.9
- gain_feedforward: float32 [1024], replicated, may hold values from 0.1 to 1.9
- gain_query: float32 [128], replicated, may hold values from 0.7 to 5
- gain_key: float32 [128], replicated, may hold values from 0.7 to 5
- query_proj: bfloat16 [1024, 2048], P('dp', 'tensor'), may hold values from -0.1875 to 0.1875
- key_proj: bfloat16 [1024, 1024], P('dp', 'tensor'), may hold values from -0.1875 to 0.1875
- value_proj: bfloat16 [1024, 1024], P('dp', 'tensor'), may hold values from -0.1875 to 0.1875
- out_proj: bfloat16 [2048, 1024], P(('tensor', 'dp')), may hold values from -3 to 3
- gate_proj: bfloat16 [1024, 3072], P('dp', 'tensor'), may hold values from -0.1875 to 0.1875
- up_proj: bfloat16 [1024, 3072], P('dp', 'tensor'), may hold values from -0.1875 to 0.1875
- down_proj: bfloat16 [3072, 1024], P(('tensor', 'dp')), may hold values from -0.21875 to 0.21875
- cotangent: bfloat16 [16384, 1024], P(('dp', 'tensor')), may hold values from -6 to 6
Outputs:
- hidden_out: bfloat16 [16384, 1024], P(('dp', 'tensor'))
- grad_hidden: float32 [16384, 1024], P(('dp', 'tensor'))
- attention_gain_grad: float32 [1024], replicated
- feedforward_gain_grad: float32 [1024], replicated
- query_gain_grad: float32 [128], replicated
- key_gain_grad: float32 [128], replicated
- query_grads: float32 [1024, 2048], P('dp', 'tensor')
- key_grads: float32 [1024, 1024], P('dp', 'tensor')
- value_grads: float32 [1024, 1024], P('dp', 'tensor')
- out_grads: float32 [2048, 1024], P(('tensor', 'dp'))
- gate_grads: float32 [1024, 3072], P('dp', 'tensor')
- up_grads: float32 [1024, 3072], P('dp', 'tensor')
- down_grads: float32 [3072, 1024], P(('tensor', 'dp'))
Inputs may be any that keep to these rules, and one draw needn't show every extreme that they name: Within each sequence of 1024 tokens the positions start at 0 and rise by one from token to token, except that they restart at 0 where a document begins; some sequence holds one document.
All inputs are finite; a program needn't handle non-finite values.
Results may differ from a plain program's by a relative error of at most 0.02.
The roundings to bfloat16 on the way count: a program that leaves them out, or rounds other values in their place, can miss the bound.
Values may be sent and summed in bfloat16 or wider, within the bound.
No kernel may reach another device: no remote copies, remote signals or barrier semaphores. Data moves between devices by JAX's collectives and lax.ppermute only.
A program may use at most 256 MiB of HBM per device.

v0:
```python
import math
import jax
import jax.numpy as jnp
from jax import lax
from jax.sharding import PartitionSpec as P

HD = 128
EPS = 1e-06
THETA = 1000000.0
BF = jnp.bfloat16
F32 = jnp.float32


def rotary_tables(positions, width):
    half_width = width // 2
    freq_index = jnp.arange(half_width).astype(F32)
    inverse_freq = jnp.exp(freq_index * (-2.0 * math.log(THETA) / width))
    angles = positions.astype(F32)[:, None] * inverse_freq[None, :]
    return (jnp.cos(angles)[:, None, :], jnp.sin(angles)[:, None, :])


def rotate(values, cosine_table, sine_table):
    half_width = values.shape[-1] // 2
    lower_half = values[..., :half_width]
    upper_half = values[..., half_width:]
    return jnp.concatenate(
        (
            lower_half * cosine_table - upper_half * sine_table,
            upper_half * cosine_table + lower_half * sine_table,
        ),
        -1,
    )


def rms_unit(values):
    inv_scale = lax.rsqrt(jnp.mean(values * values, -1, keepdims=True) + EPS)
    return (values * inv_scale, inv_scale)


def rms_back(grad_out, gain_vec, unit_vals, inv_scale):
    scaled_grad = grad_out * gain_vec
    return inv_scale * (
        scaled_grad - unit_vals * jnp.mean(scaled_grad * unit_vals, -1, keepdims=True)
    )


def matmul(left, right):
    return jnp.dot(left, right, preferred_element_type=F32)


def contract_rows(left, right):
    return lax.dot_general(left, right, (((0,), (0,)), ((), ())), preferred_element_type=F32)


def contract_cols(left, right):
    return lax.dot_general(left, right, (((1,), (1,)), ((), ())), preferred_element_type=F32)


def attend(query_b, key_b, value_b):
    length = query_b.shape[0]
    block_rows = min(length, 512)
    block_count = length // block_rows
    scale_qk = 1.0 / math.sqrt(query_b.shape[-1])
    outputs = []
    log_sums = []
    for block in range(block_count):
        row_start = block * block_rows
        key_end = row_start + block_rows
        query_block = query_b[row_start:key_end]
        scores = (
            jnp.einsum("qgrd,kgd->grqk", query_block, key_b[:key_end], preferred_element_type=F32)
            * scale_qk
        )
        causal = (row_start + jnp.arange(block_rows, dtype=jnp.int32))[:, None] >= jnp.arange(
            key_end, dtype=jnp.int32
        )[None, :]
        scores = jnp.where(causal, scores, -jnp.inf)
        top_score = jnp.max(scores, -1, keepdims=True)
        shifted = jnp.exp(scores - top_score)
        sum_exp = jnp.sum(shifted, -1, keepdims=True)
        probs_b = (shifted / sum_exp).astype(BF)
        outputs.append(
            jnp.einsum("grqk,kgd->qgrd", probs_b, value_b[:key_end], preferred_element_type=F32)
        )
        log_sums.append(top_score + jnp.log(sum_exp))
    return (jnp.concatenate(outputs, 0), log_sums)


def attend_back(query_b, key_b, value_b, grad_b, log_sums):
    length = query_b.shape[0]
    block_rows = min(length, 512)
    block_count = length // block_rows
    scale_qk = 1.0 / math.sqrt(query_b.shape[-1])
    key_acc = jnp.zeros(key_b.shape, F32)
    value_acc = jnp.zeros(key_b.shape, F32)
    grad_queries = []
    for block in range(block_count):
        row_start = block * block_rows
        key_end = row_start + block_rows
        query_block = query_b[row_start:key_end]
        grad_block = grad_b[row_start:key_end]
        keys_seen = key_b[:key_end]
        scores = (
            jnp.einsum("qgrd,kgd->grqk", query_block, keys_seen, preferred_element_type=F32)
            * scale_qk
        )
        causal = (row_start + jnp.arange(block_rows, dtype=jnp.int32))[:, None] >= jnp.arange(
            key_end, dtype=jnp.int32
        )[None, :]
        scores = jnp.where(causal, scores, -jnp.inf)
        probs = jnp.exp(scores - log_sums[block])
        probs_b = probs.astype(BF)
        grad_probs = jnp.einsum(
            "qgrd,kgd->grqk", grad_block, value_b[:key_end], preferred_element_type=F32
        )
        row_dot = jnp.sum(probs * grad_probs, -1, keepdims=True)
        grad_scores_b = (probs * (grad_probs - row_dot)).astype(BF)
        grad_queries.append(
            jnp.einsum("grqk,kgd->qgrd", grad_scores_b, keys_seen, preferred_element_type=F32)
            * scale_qk
        )
        key_acc = key_acc.at[:key_end].add(
            jnp.einsum("grqk,qgrd->kgd", grad_scores_b, query_block, preferred_element_type=F32)
            * scale_qk
        )
        value_acc = value_acc.at[:key_end].add(
            jnp.einsum("grqk,qgrd->kgd", probs_b, grad_block, preferred_element_type=F32)
        )
    return (jnp.concatenate(grad_queries, 0), key_acc, value_acc)


def all_sum(value, sizes):
    for axis, size in sizes:
        if size & size - 1:
            value = lax.psum(value, axis)
            continue
        step = 1
        while step < size:
            value = value + lax.ppermute(value, axis, [(i, i ^ step) for i in range(size)])
            step *= 2
    return value


def make_local(n_dp, n_tensor):
    paired = n_tensor == 2
    swap = [(0, 1), (1, 0)]

    def gather_rows(own):
        if paired:
            return jnp.concatenate((own, lax.ppermute(own, "tensor", swap)), 0)
        return lax.all_gather(own, "tensor", axis=0, tiled=True)

    def to_sequence(rows):
        if not paired:
            return rows
        half = rows.shape[0] // 2
        first = lax.axis_index("tensor") == 0
        return jnp.concatenate(
            (
                jnp.where(first, rows[:half], rows[half:]),
                jnp.where(first, rows[half:], rows[:half]),
            ),
            0,
        )

    def scatter_rows(part, operand):
        if paired:
            half = operand[0].shape[0] // 2
            sent = part(*(o[half:] for o in operand)).astype(BF)
            got = lax.ppermute(sent, "tensor", swap)
            return part(*(o[:half] for o in operand)) + got.astype(F32)
        return lax.psum_scatter(
            part(*operand).astype(BF), "tensor", scatter_dimension=0, tiled=True
        ).astype(F32)

    def local(
        hidden_in,
        positions,
        gain_attention,
        gain_feedforward,
        gain_query,
        gain_key,
        query_proj,
        key_proj,
        value_proj,
        out_proj,
        gate_proj,
        up_proj,
        down_proj,
        cotangent,
    ):
        length = positions.shape[0]
        own = hidden_in.shape[0]
        width = hidden_in.shape[1]
        heads_here = query_proj.shape[1] // HD
        groups_here = key_proj.shape[1] // HD
        width_query = heads_here * HD
        width_key = groups_here * HD
        width_qkv = width_query + 2 * width_key
        units = gate_proj.shape[1]
        shard_rows = query_proj.shape[0]
        shard_attn = jnp.concatenate(
            (query_proj, key_proj, value_proj, out_proj.reshape(shard_rows, -1)), 1
        )
        shard_mlp = jnp.concatenate((gate_proj, up_proj, down_proj.reshape(shard_rows, -1)), 1)
        full_attn = lax.all_gather(shard_attn, "dp", axis=0, tiled=True)
        full_mlp = lax.all_gather(shard_mlp, "dp", axis=0, tiled=True)
        proj_qkv = full_attn[:, :width_qkv]
        full_out = full_attn[:, width_qkv:].reshape(-1, width)
        full_gateup = full_mlp[:, : 2 * units]
        full_down = full_mlp[:, 2 * units :].reshape(-1, width)
        rows_hidden = gather_rows(hidden_in)
        rows_cot = gather_rows(cotangent)
        cosine_table, sine_table = rotary_tables(positions, HD)
        unit_rows, scale_rows = rms_unit(rows_hidden.astype(F32))
        rows_attn = (unit_rows * gain_attention).astype(BF)
        if paired:
            hidden_f, unit_attn, scale_attn = (
                hidden_in.astype(F32),
                unit_rows[:own],
                scale_rows[:own],
            )
        else:
            hidden_f = hidden_in.astype(F32)
            unit_attn, scale_attn = rms_unit(hidden_f)
        projected = to_sequence(matmul(rows_attn, proj_qkv))
        query_raw = projected[:, :width_query].reshape(length, heads_here, HD)
        key_raw = projected[:, width_query : width_query + width_key].reshape(
            length, groups_here, HD
        )
        value_b = (
            projected[:, width_query + width_key :].astype(BF).reshape(length, groups_here, HD)
        )
        query_unit, query_scale = rms_unit(query_raw)
        key_unit, key_scale = rms_unit(key_raw)
        query_b = (
            rotate(query_unit * gain_query, cosine_table, sine_table)
            .astype(BF)
            .reshape(length, groups_here, heads_here // groups_here, HD)
        )
        key_b = rotate(key_unit * gain_key, cosine_table, sine_table).astype(BF)
        heads_out, log_sums = attend(query_b, key_b, value_b)
        heads_b = to_sequence(heads_out.reshape(length, width_query).astype(BF))
        resid = hidden_f + scatter_rows(lambda h: matmul(h, full_out), (heads_b,))
        unit_mlp, scale_mlp = rms_unit(resid)
        rows_mlp = gather_rows((unit_mlp * gain_feedforward).astype(BF))
        gate_val = matmul(rows_mlp, full_gateup[:, :units])
        up_val = matmul(rows_mlp, full_gateup[:, units:])
        sigmoid_gate = jax.nn.sigmoid(gate_val)
        active_b = (gate_val * sigmoid_gate * up_val).astype(BF)
        output_b = (resid + scatter_rows(lambda a: matmul(a, full_down), (active_b,))).astype(BF)
        grad_active = contract_cols(rows_cot, full_down)
        grad_gate_b = (
            grad_active * up_val * sigmoid_gate * (1.0 + gate_val * (1.0 - sigmoid_gate))
        ).astype(BF)
        grad_up_b = (grad_active * gate_val * sigmoid_gate).astype(BF)
        grad_normed_mlp = scatter_rows(
            lambda g, u: contract_cols(g, full_gateup[:, :units])
            + contract_cols(u, full_gateup[:, units:]),
            (grad_gate_b, grad_up_b),
        )
        grad_mlp_w = jnp.concatenate(
            (
                contract_rows(rows_mlp, grad_gate_b).astype(BF),
                contract_rows(rows_mlp, grad_up_b).astype(BF),
                contract_rows(active_b, rows_cot).astype(BF).reshape(width, -1),
            ),
            1,
        )
        sent_mlp = lax.psum_scatter(grad_mlp_w, "dp", scatter_dimension=0, tiled=True)
        term_feedforward = jnp.sum(grad_normed_mlp * unit_mlp, 0)
        grad_resid = cotangent.astype(F32) + rms_back(
            grad_normed_mlp, gain_feedforward, unit_mlp, scale_mlp
        )
        rows_resid = gather_rows(grad_resid.astype(BF))
        grad_heads_b = to_sequence(contract_cols(rows_resid, full_out).astype(BF)).reshape(
            length, groups_here, heads_here // groups_here, HD
        )
        grad_qrot, grad_krot, grad_value = attend_back(
            query_b, key_b, value_b, grad_heads_b, log_sums
        )
        grad_qnormed = rotate(grad_qrot.reshape(length, heads_here, HD), cosine_table, -sine_table)
        grad_knormed = rotate(grad_krot, cosine_table, -sine_table)
        term_query = jnp.sum(grad_qnormed * query_unit, (0, 1))
        term_key = jnp.sum(grad_knormed * key_unit, (0, 1))
        grad_qkv_b = to_sequence(
            jnp.concatenate(
                (
                    rms_back(grad_qnormed, gain_query, query_unit, query_scale).reshape(
                        length, width_query
                    ),
                    rms_back(grad_knormed, gain_key, key_unit, key_scale).reshape(
                        length, width_key
                    ),
                    grad_value.reshape(length, width_key),
                ),
                1,
            ).astype(BF)
        )
        grad_attn_w = jnp.concatenate(
            (
                contract_rows(rows_attn, grad_qkv_b).astype(BF),
                contract_rows(heads_b, rows_resid).astype(BF).reshape(width, -1),
            ),
            1,
        )
        sent_attn = lax.psum_scatter(grad_attn_w, "dp", scatter_dimension=0, tiled=True)
        grad_normed_attn = scatter_rows(lambda g: contract_cols(g, proj_qkv), (grad_qkv_b,))
        term_attention = jnp.sum(grad_normed_attn * unit_attn, 0)
        grad_hidden = grad_resid + rms_back(grad_normed_attn, gain_attention, unit_attn, scale_attn)
        terms = all_sum(
            jnp.concatenate((term_attention, term_feedforward, term_query, term_key)).reshape(
                -1, HD
            ),
            (("tensor", n_tensor), ("dp", n_dp)),
        ).reshape(-1)
        sent_attn = sent_attn.astype(F32)
        sent_mlp = sent_mlp.astype(F32)
        return (
            output_b,
            grad_hidden,
            terms[:width],
            terms[width : 2 * width],
            terms[2 * width : 2 * width + HD],
            terms[2 * width + HD :],
            sent_attn[:, :width_query],
            sent_attn[:, width_query : width_query + width_key],
            sent_attn[:, width_query + width_key : width_qkv],
            sent_attn[:, width_qkv:].reshape(out_proj.shape),
            sent_mlp[:, :units],
            sent_mlp[:, units : 2 * units],
            sent_mlp[:, 2 * units :].reshape(down_proj.shape),
        )

    return local


def solution(mesh):
    rows = P(("dp", "tensor"), None)
    cut = P("dp", "tensor")
    stacked = P(("tensor", "dp"), None)
    return jax.shard_map(
        make_local(mesh.shape["dp"], mesh.shape["tensor"]),
        mesh=mesh,
        in_specs=(
            rows,
            P("dp"),
            P(),
            P(),
            P(),
            P(),
            cut,
            cut,
            cut,
            stacked,
            cut,
            cut,
            stacked,
            rows,
        ),
        out_specs=(rows, rows, P(), P(), P(), P(), cut, cut, cut, stacked, cut, cut, stacked),
        check_vma=False,
    )
```

profile of v0, /device:TPU:0, one launch (start us, length us, event | category | flops | bytes accessed | tf_op | source)
XLA Modules:
  0.0 633.6 jit_solution(4155793221985874017)
XLA Ops:
  12.2 3.1 collective-permute-start
  17.3 2.9 fusion.117
  20.3 18.2 %collective-permute-done = bf16[512,1024]{1,0:T(8,128)(2,1)S(1)} collective-permute-done((bf16[512,1024]{1,0:T(8,128)(2,1)S(1)}, bf16[512,1024]{1,0:T(8,128)(2,1)S(1)}, u32[]{:S(2)}, u32[]{:S(2)}) %collective-permute-start) | collective-permute-done | bytes 1048608 | tf_op jit(solution)/shard_map/ppermute | solution.py:150
  39.0 36.1 %all-gather.3.cloned.1.call-done = bf16[1024,3072]{1,0:T(8,128)(2,1)} async-done(((bf16[64,3072]{1,0:T(8,128)(2,1)}), bf16[1024,3072]{1,0:T(8,128)(2,1)}) %all-gather.3.cloned.1.call-update) | async-done | bytes 6291472 | tf_op jit(solution)/shard_map/all_gather | solution.py:206
  75.0 10.0 %fusion.36 = f32[1024,2048]{1,0:T(8,128)} fusion(bf16[1024,3072]{1,0:T(8,128)(2,1)} %all-gather.3.cloned.1.call-done, f32[1024]{0:T(1024)S(1)} %copy-done.74, f32[1024]{0:T(1024)S(1)} %add_rsqrt_fusion.2, bf16[512,1024]{1,0:T(8,128)(2,1)S(1)} %collective-permute-done, bf16[512,1024]{1,0:T(8,128)(2,1)S(1)} %copy-done.40), kind=kOutput, calls=%fused_computation.77 | convolution fusion | flops 4302307328 | bytes 14688256 | tf_op jit(solution)/shard_map/dot_general | solution.py:48
  85.0 4.3 slice_select_fusion.1
  89.4 3.3 fusion.5
  107.3 3.7 multiply_reduce_fusion.8
  125.7 7.5 %fusion.135 = (f32[4,2,512]{2,1,0:T(2,128)S(1)}, f32[4,2,512,1024]{2,3,1,0:T(8,128)}) fusion(bf16[512,4,2,128]{3,0,2,1:T(8,128)(2,1)S(1)} %bitcast.234, bf16[1024,4,64]{2,0,1:T(8,128)(2,1)S(1)} %get-tuple-element.107, bf16[1024,4,64]{2,0,1:T(8,128)(2,1)S(1)} %get-tuple-element.106, pred[512,1024]{0,1:T(8,128)(4,1)S(1)} %copy-done.58), kind=kOutput, calls=%fused_computation.226 | convolution fusion | flops 1088417792 | bytes 19415040 | tf_op jit(solution)/shard_map/qgrd,kgd->grqk/dot_general | solution.py:71
  133.2 8.3 %fusion.3 = f32[4,2,512]{2,1,0:T(2,128)S(1)} fusion(f32[4,2,512,1024]{2,3,1,0:T(8,128)} %get-tuple-element.129, f32[4,2,512]{2,1,0:T(2,128)S(1)} %get-tuple-element.128), kind=kLoop, calls=%fused_computation.9 | loop fusion | flops 8384512 | bytes 16809984 | tf_op jit(solution)/shard_map/reduce_sum | solution.py:80
  141.6 7.8 %fusion.80 = bf16[4,128,2,512]{3,1,2,0:T(8,128)(2,1)S(1)} fusion(f32[4,2,512,1024]{2,3,1,0:T(8,128)} %get-tuple-element.129, f32[4,2,512]{2,1,0:T(2,128)S(1)} %fusion.3, f32[4,2,512]{2,1,0:T(2,128)S(1)} %get-tuple-element.128, bf16[1024,4,128,1]{2,1,0,3:T(4,128)(2,1)S(1)} %bitcast.237), kind=kOutput, calls=%fused_computation.156 | convolution fusion | flops 1086849024 | bytes 18907136 | tf_op jit(solution)/shard_map/grqk,kgd->qgrd/dot_general | solution.py:83
  151.8 3.6 fusion.84
  157.6 24.0 %collective-permute-done.1 = bf16[512,1024]{1,0:T(8,128)(2,1)S(1)} collective-permute-done((bf16[512,1024]{1,0:T(8,128)(2,1)S(1)}, bf16[512,1024]{1,0:T(8,128)(2,1)S(1)}, u32[]{:S(2)}, u32[]{:S(2)}) %collective-permute-start.1) | collective-permute-done | bytes 1048608 | tf_op jit(solution)/shard_map/ppermute | solution.py:170
  181.6 3.2 multiply_reduce_fusion.7
  188.9 15.2 %collective-permute-done.4 = bf16[512,1024]{1,0:T(8,128)(2,1)S(1)} collective-permute-done((bf16[512,1024]{1,0:T(8,128)(2,1)S(1)}, bf16[512,1024]{1,0:T(8,128)(2,1)S(1)}, u32[]{:S(2)}, u32[]{:S(2)}) %collective-permute-start.4) | collective-permute-done | bytes 1048608 | tf_op jit(solution)/shard_map/ppermute | solution.py:150
  205.1 3.7 slice.345
  208.8 5.9 reshape.389
  214.7 8.8 %fusion.136 = f32[1024,1536]{1,0:T(8,128)} fusion(bf16[1024,1024]{1,0:T(8,128)(2,1)} %constant_dynamic-update-slice_fusion, bf16[1536,1024]{1,0:T(8,128)(2,1)} %reshape.389), kind=kOutput, calls=%fused_computation.227 | convolution fusion | flops 3221225472 | bytes 11534336 | tf_op jit(solution)/shard_map/dot_general | solution.py:56
  225.9 8.6 %fusion.42 = f32[1024,1536]{1,0:T(8,128)} fusion(bf16[1024,4608]{1,0:T(8,128)(2,1)} %all-gather.5.cloned.1.call-done, bf16[512,1024]{1,0:T(8,128)(2,1)} %collective-permute-done.2, bf16[512,1024]{1,0:T(8,128)(2,1)} %multiply_convert_fusion.4), kind=kOutput, calls=%fused_computation.83 | convolution fusion | flops 3225419776 | bytes 11534336 | tf_op jit(solution)/shard_map/dot_general | solution.py:48
  234.5 10.6 %multiply_convert_fusion.1 = (bf16[1024,1536]{1,0:T(8,128)(2,1)S(1)}, bf16[1024,1536]{1,0:T(8,128)(2,1)}, bf16[1024,1536]{1,0:T(8,128)(2,1)S(1)}) fusion(f32[1024,1536]{1,0:T(8,128)} %fusion.136, f32[1024,1536]{1,0:T(8,128)} %fusion.42, bf16[1024,4608]{1,0:T(8,128)(2,1)S(1)} %bitcast.242, bf16[512,1024]{1,0:T(8,128)(2,1)} %collective-permute-done.2, ...), kind=kOutput, calls=%fused_computation.34 | convolution fusion | flops 3250585600 | bytes 27262976 | tf_op jit(solution)/shard_map/dot_general | solution.py:48
  252.2 21.1 %collective-permute-done.5 = bf16[512,1024]{1,0:T(8,128)(2,1)S(1)} collective-permute-done((bf16[512,1024]{1,0:T(8,128)(2,1)S(1)}, bf16[512,1024]{1,0:T(8,128)(2,1)S(1)}, u32[]{:S(2)}, u32[]{:S(2)}) %collective-permute-start.5) | collective-permute-done | bytes 1048608 | tf_op jit(solution)/shard_map/ppermute | solution.py:170
  273.3 2.8 multiply_reduce_fusion.2
  281.0 20.6 %collective-permute-done.6 = bf16[512,1024]{1,0:T(8,128)(2,1)S(1)} collective-permute-done((bf16[512,1024]{1,0:T(8,128)(2,1)}, bf16[512,1024]{1,0:T(8,128)(2,1)S(1)}, u32[]{:S(2)}, u32[]{:S(2)}) %collective-permute-start.6) | collective-permute-done | bytes 1048608 | tf_op jit(solution)/shard_map/ppermute | solution.py:150
  301.6 4.7 convolution_convert_fusion.3
  309.4 2.7 fusion.10
  319.2 11.2 %fusion = (f32[4,2,512]{2,1,0:T(2,128)}, f32[4,1024,512,2]{2,1,3,0:T(8,128)}) fusion(f32[4,2,512,1024]{2,3,1,0:T(8,128)S(1)} %bitcast.217, f32[4,2,512]{2,1,0:T(2,128)} %bitcast.246, bf16[512,4,2,128]{0,3,2,1:T(8,128)(2,1)} %bitcast.230, bf16[1024,4,128,1]{2,1,0,3:T(4,128)(2,1)} %bitcast.236), kind=kOutput, calls=%fused_computation.2 | convolution fusion | flops 1086320640 | bytes 35684352 | tf_op jit(solution)/shard_map/qgrd,kgd->grqk/dot_general | solution.py:113
  330.5 8.4 %fusion.2 = bf16[4,2,512,1024]{2,3,1,0:T(8,128)(2,1)S(1)} fusion(f32[4,1024,512,2]{2,1,3,0:T(8,128)} %get-tuple-element.136, f32[4,2,512,1024]{2,3,1,0:T(8,128)S(1)} %bitcast.217, f32[4,2,512]{2,1,0:T(2,128)} %get-tuple-element.135, f32[4,2,512]{2,1,0:T(2,128)} %bitcast.247), kind=kLoop, calls=%fused_computation.4 | loop fusion | flops 16777216 | bytes 41975808 | tf_op jit(solution)/shard_map/convert_element_type | solution.py:117
  344.5 3.9 copy.226
  348.4 2.7 copy.227
  351.2 4.1 multiply_subtract_fusion
  356.0 17.1 %multiply_reduce_fusion = (f32[1024,8]{1,0:T(8,128)S(1)}, f32[1024,8,128]{2,1,0:T(8,128)}) fusion(f32[1024,8,128]{2,1,0:T(8,128)S(1)} %bitcast.221, f32[128]{0:T(128)S(1)} %copy-done.71, f32[1024,8]{1,0:T(8,128)S(1)} %copy-done.27, f32[1024,8,64]{2,1,0:T(8,128)S(1)} %get-tuple-element.89, f32[1024,8,64]{2,1,0:T(8,128)S(1)} %get-tuple-element.88), kind=kLoop, calls=%fused_computation.57 | loop fusion | flops 5234688 | bytes 12648960 | tf_op jit(solution)/shard_map/reduce_sum | solution.py:43
  377.8 2.8 fusion.111
  381.7 9.9 %fusion.59 = bf16[1024,4,128]{0,2,1:T(8,128)(2,1)} fusion(f32[512,4,128]{0,2,1:T(8,128)} %fusion.100, bf16[512,4,2,128]{0,3,2,1:T(8,128)(2,1)S(1)} %bitcast.231, f32[4,2,512,1024]{2,3,1,0:T(8,128)} %get-tuple-element.129, f32[4,2,512]{2,1,0:T(2,128)S(1)} %bitcast.248), kind=kOutput, calls=%fused_computation.112 | convolution fusion | flops 1083179008 | bytes 19939328 | tf_op jit(solution)/shard_map/grqk,qgrd->kgd/dot_general | solution.py:127
  398.5 7.0 %fusion.22 = (f32[1024]{0:T(1024)S(1)}, bf16[1024,1024]{1,0:T(8,128)(2,1)S(1)}) fusion(f32[128,8,8,128]{3,2,1,0:T(8,128)} %bitcast.222, f32[128,8,8,128]{3,2,1,0:T(8,128)S(1)} %bitcast.225, f32[512,2048]{1,0:T(8,128)S(1)} %copy-done.4, f32[512,2048]{1,0:T(8,128)S(1)} %copy-done.2, f32[128,8,8,128]{3,2,1,0:T(8,128)S(1)} %bitcast.224, ...), kind=kLoop, calls=%fused_computation.48 | loop fusion | flops 11533312 | bytes 23076864 | tf_op jit(solution)/shard_map/reduce_sum | solution.py:284
  411.7 4.5 fusion.60
  416.3 5.3 fusion.29
  421.5 3.2 pad_maximum_fusion.2
  426.6 6.7 %convolution_convert_fusion = bf16[1536,1024]{1,0:T(8,128)(2,1)} fusion(bf16[1024,1536]{1,0:T(8,128)(2,1)S(1)} %copy-done.84, bf16[1024,1024]{1,0:T(8,128)(2,1)} %constant_dynamic-update-slice_fusion), kind=kOutput, calls=%fused_computation.70 | convolution fusion | flops 3222798336 | bytes 8388608 | tf_op jit(solution)/shard_map/dot_general | solution.py:52
  433.3 4.6 reshape.393
  437.9 6.5 %convolution_convert_fusion.2 = bf16[1024,1536]{1,0:T(8,128)(2,1)S(1)} fusion(bf16[1024,1536]{1,0:T(8,128)(2,1)} %copy-done.83, bf16[512,1024]{1,0:T(8,128)(2,1)} %collective-permute-done.2, bf16[512,1024]{1,0:T(8,128)(2,1)} %multiply_convert_fusion.4), kind=kOutput, calls=%fused_computation.72 | convolution fusion | flops 3226992640 | bytes 8388608 | tf_op jit(solution)/shard_map/dot_general | solution.py:52
  444.4 5.4 convolution_convert_fusion.1
  449.9 5.3 pad_maximum_fusion.1
  456.8 4.7 fusion.87
  467.8 19.8 %collective-permute-done.7 = bf16[512,1024]{1,0:T(8,128)(2,1)S(1)} collective-permute-done((bf16[512,1024]{1,0:T(8,128)(2,1)S(1)}, bf16[512,1024]{1,0:T(8,128)(2,1)S(1)}, u32[]{:S(2)}, u32[]{:S(2)}) %collective-permute-start.7) | collective-permute-done | bytes 1048608 | tf_op jit(solution)/shard_map/ppermute | solution.py:170
  487.6 2.7 multiply_reduce_fusion.3
  491.9 15.5 %collective-permute-done.8 = f32[18,128]{1,0:T(8,128)S(1)} collective-permute-done((f32[18,128]{1,0:T(8,128)S(1)}, f32[18,128]{1,0:T(8,128)S(1)}, u32[]{:S(2)}, u32[]{:S(2)}) %collective-permute-start.8) | collective-permute-done | bytes 9248 | tf_op jit(solution)/shard_map/ppermute | solution.py:139
  510.6 2.8 add_convert_fusion.2
  526.2 97.4 %reduce-scatter.5.cloned.1.call-done = bf16[64,4608]{1,0:T(8,128)(2,1)} async-done(((bf16[1024,4608]{1,0:T(8,128)(2,1)}), bf16[64,4608]{1,0:T(8,128)(2,1)}) %reduce-scatter.5.cloned.1.call-update) | async-done | bytes 589840 | tf_op jit(solution)/shard_map/reduce_scatter | solution.py:270
  (330 shorter events, 125.8 us)
Async XLA Ops:
  7.2 67.8 %all-gather.3.cloned.1.call-start = ((), (), s32[]{:S(2)}) async-start(), calls=%async_computation.2 | async-start | bytes 6684672 | tf_op jit(solution)/shard_map/all_gather | solution.py:206
  9.2 195.9 %all-gather.5.cloned.1.call-start = ((), (), s32[]{:S(2)}) async-start(), calls=%async_computation.3 | async-start | bytes 10027008 | tf_op jit(solution)/shard_map/all_gather | solution.py:207
  10.3 64.8 %copy-start.74 = (f32[1024]{0:T(1024)S(1)}, f32[1024]{0:T(1024)}, u32[]{:S(2)}) copy-start(f32[1024]{0:T(1024)} %param.28) | copy-start | bytes 12292
  12.2 510.6 %reduce-scatter.3.cloned.1.call-start = ((), (), s32[]{:S(2)}) async-start(), calls=%async_computation.4 | async-start | bytes 6684672 | tf_op jit(solution)/shard_map/reduce_scatter | solution.py:307
  12.2 26.2 %collective-permute-start = (bf16[512,1024]{1,0:T(8,128)(2,1)S(1)}, bf16[512,1024]{1,0:T(8,128)(2,1)S(1)}, u32[]{:S(2)}, u32[]{:S(2)}) collective-permute-start(bf16[512,1024]{1,0:T(8,128)(2,1)S(1)} %copy-done.40), channel_id=1, source_target_pairs={{0,1},{1,0},{2,3},{3,2},{4,5},{5,4},{6,7},{7,6},{8,9},{9,8},{10,11... | collective-permute-start | bytes 3145736 | tf_op jit(solution)/shard_map/ppermute | solution.py:150
  20.3 79.7 %copy-start.15 = (f32[1024,64]{1,0:T(8,128)}, f32[1024,64]{1,0:T(8,128)S(1)}, u32[]{:S(2)}) copy-start(f32[1024,64]{1,0:T(8,128)S(1)} %get-tuple-element.125) | copy-start | bytes 786436
  20.3 79.7 %copy-start.34 = (f32[1024,64]{1,0:T(8,128)}, f32[1024,64]{1,0:T(8,128)S(1)}, u32[]{:S(2)}) copy-start(f32[1024,64]{1,0:T(8,128)S(1)} %get-tuple-element.124) | copy-start | bytes 786436
  38.5 46.6 %copy-start.44 = (bf16[512,1024]{1,0:T(8,128)(2,1)}, bf16[512,1024]{1,0:T(8,128)(2,1)S(1)}, u32[]{:S(2)}) copy-start(bf16[512,1024]{1,0:T(8,128)(2,1)S(1)} %collective-permute-done) | copy-start | bytes 3145732
  39.0 46.1 %copy-start.67 = (f32[1024]{0:T(1024)}, f32[1024]{0:T(1024)S(1)}, u32[]{:S(2)}) copy-start(f32[1024]{0:T(1024)S(1)} %add_rsqrt_fusion.2) | copy-start | bytes 12292
  89.4 15.4 %copy-start.1 = (f32[512,2048]{1,0:T(8,128)}, f32[512,2048]{1,0:T(8,128)S(1)}, u32[]{:S(2)}) copy-start(f32[512,2048]{1,0:T(8,128)S(1)} %get-tuple-element.90) | copy-start | bytes 12582916
  89.4 15.4 %copy-start.3 = (f32[512,2048]{1,0:T(8,128)}, f32[512,2048]{1,0:T(8,128)S(1)}, u32[]{:S(2)}) copy-start(f32[512,2048]{1,0:T(8,128)S(1)} %get-tuple-element.91) | copy-start | bytes 12582916
  105.1 12.8 %copy-start.8 = (f32[1024,512]{1,0:T(8,128)}, f32[1024,512]{1,0:T(8,128)S(1)}, u32[]{:S(2)}) copy-start(f32[1024,512]{1,0:T(8,128)S(1)} %fusion.50) | copy-start | bytes 6291460
  117.9 161.4 %copy-start.60 = (f32[1024,4]{0,1:T(4,128)}, f32[1024,4]{0,1:T(4,128)S(1)}, u32[]{:S(2)}) copy-start(f32[1024,4]{0,1:T(4,128)S(1)} %add_rsqrt_fusion.1) | copy-start | bytes 49156
  133.2 16.2 %slice-start = ((s8[8388608]{0:T(1024)(128)(4,1)}), s8[4194304]{0:T(1024)(128)(4,1)S(1)}, s32[]{:S(2)}) async-start(s8[8388608]{0:T(1024)(128)(4,1)} %bitcast.212), calls=%async_computation.6 | async-start | bytes 8388608
  151.8 29.8 %copy-start.79 = (bf16[4,128,2,512]{3,1,2,0:T(8,128)(2,1)}, bf16[4,128,2,512]{3,1,2,0:T(8,128)(2,1)S(1)}, u32[]{:S(2)}) copy-start(bf16[4,128,2,512]{3,1,2,0:T(8,128)(2,1)S(1)} %get-tuple-element.110) | copy-start | bytes 3145732
  151.8 29.8 %copy-start.41 = (bf16[512,1024]{1,0:T(8,128)(2,1)S(1)}, bf16[512,1024]{1,0:T(8,128)(2,1)}, u32[]{:S(2)}) copy-start(bf16[512,1024]{1,0:T(8,128)(2,1)} %param.26) | copy-start | bytes 3145732
  155.5 26.1 %collective-permute-start.1 = (bf16[512,1024]{1,0:T(8,128)(2,1)S(1)}, bf16[512,1024]{1,0:T(8,128)(2,1)S(1)}, u32[]{:S(2)}, u32[]{:S(2)}) collective-permute-start(bf16[512,1024]{1,0:T(8,128)(2,1)S(1)} %fusion.84), channel_id=1, source_target_pairs={{0,1},{1,0},{2,3},{3,2},{4,5},{5,4},{6,7},{7,6},{8,9},{9,8},{10,11... | collective-permute-start | bytes 3145736 | tf_op jit(solution)/shard_map/ppermute | solution.py:170
  157.1 46.9 %collective-permute-start.4 = (bf16[512,1024]{1,0:T(8,128)(2,1)S(1)}, bf16[512,1024]{1,0:T(8,128)(2,1)S(1)}, u32[]{:S(2)}, u32[]{:S(2)}) collective-permute-start(bf16[512,1024]{1,0:T(8,128)(2,1)S(1)} %copy-done.23), channel_id=1, source_target_pairs={{0,1},{1,0},{2,3},{3,2},{4,5},{5,4},{6,7},{7,6},{8,9},{9,8},{10,11... | collective-permute-start | bytes 3145736 | tf_op jit(solution)/shard_map/ppermute | solution.py:150
  184.7 91.4 %copy-start.10 = (f32[512,1024]{1,0:T(8,128)}, f32[512,1024]{1,0:T(8,128)S(1)}, u32[]{:S(2)}) copy-start(f32[512,1024]{1,0:T(8,128)S(1)} %get-tuple-element.131) | copy-start | bytes 6291460
  184.7 91.4 %copy-start.65 = (f32[512]{0:T(512)}, f32[512]{0:T(512)S(1)}, u32[]{:S(2)}) copy-start(f32[512]{0:T(512)S(1)} %add_rsqrt_fusion.3) | copy-start | bytes 6148
  186.3 39.6 %collective-permute-start.2 = (bf16[512,1024]{1,0:T(8,128)(2,1)}, bf16[512,1024]{1,0:T(8,128)(2,1)}, u32[]{:S(2)}, u32[]{:S(2)}) collective-permute-start(bf16[512,1024]{1,0:T(8,128)(2,1)} %multiply_convert_fusion.4), channel_id=1, source_target_pairs={{0,1},{1,0},{2,3},{3,2},{4,5},{5,4},{6,7},{7,6},{8,9},{9,8},{10,11... | collective-permute-start | bytes 3145736 | tf_op jit(solution)/shard_map/ppermute | solution.py:150
  214.7 19.8 %slice-start.11 = ((s8[9437184]{0:T(1024)(128)(4,1)}), s8[4194304]{0:T(1024)(128)(4,1)S(1)}, s32[]{:S(2)}) async-start(s8[9437184]{0:T(1024)(128)(4,1)} %bitcast.241), calls=%async_computation.17 | async-start | bytes 8388608
  214.7 19.8 %slice-start.12 = ((s8[9437184]{0:T(1024)(128)(4,1)}), s8[4194304]{0:T(1024)(128)(4,1)S(1)}, s32[]{:S(2)}) async-start(s8[9437184]{0:T(1024)(128)(4,1)} %bitcast.241), calls=%async_computation.18 | async-start | bytes 8388608
  223.5 11.0 %slice-start.13 = ((s8[9437184]{0:T(1024)(128)(4,1)}), s8[1048576]{0:T(1024)(128)(4,1)S(1)}, s32[]{:S(2)}) async-start(s8[9437184]{0:T(1024)(128)(4,1)} %bitcast.241), calls=%async_computation.19 | async-start | bytes 2097152
  245.1 28.2 %copy-start.83 = (bf16[1024,1536]{1,0:T(8,128)(2,1)}, bf16[1024,1536]{1,0:T(8,128)(2,1)S(1)}, u32[]{:S(2)}) copy-start(bf16[1024,1536]{1,0:T(8,128)(2,1)S(1)} %get-tuple-element.85) | copy-start | bytes 9437188
  248.8 24.5 %collective-permute-start.5 = (bf16[512,1024]{1,0:T(8,128)(2,1)S(1)}, bf16[512,1024]{1,0:T(8,128)(2,1)S(1)}, u32[]{:S(2)}, u32[]{:S(2)}) collective-permute-start(bf16[512,1024]{1,0:T(8,128)(2,1)S(1)} %add_convert_fusion.1), channel_id=1, source_target_pairs={{0,1},{1,0},{2,3},{3,2},{4,5},{5,4},{6,7},{7,6},{8,9},{9,8},{10,11... | collective-permute-start | bytes 3145736 | tf_op jit(solution)/shard_map/ppermute | solution.py:170
  252.2 24.0 %copy-start.24 = (bf16[512,1024]{1,0:T(8,128)(2,1)S(1)}, bf16[512,1024]{1,0:T(8,128)(2,1)}, u32[]{:S(2)}) copy-start(bf16[512,1024]{1,0:T(8,128)(2,1)} %param.39) | copy-start | bytes 3145732
  277.8 23.8 %collective-permute-start.6 = (bf16[512,1024]{1,0:T(8,128)(2,1)}, bf16[512,1024]{1,0:T(8,128)(2,1)S(1)}, u32[]{:S(2)}, u32[]{:S(2)}) collective-permute-start(bf16[512,1024]{1,0:T(8,128)(2,1)} %fusion.128), channel_id=1, source_target_pairs={{0,1},{1,0},{2,3},{3,2},{4,5},{5,4},{6,7},{7,6},{8,9},{9,8},{10,11... | collective-permute-start | bytes 3145736 | tf_op jit(solution)/shard_map/ppermute | solution.py:150
  280.3 27.1 %slice-start.2 = ((s8[8388608]{0:T(1024)(128)(4,1)}), s8[4194304]{0:T(1024)(128)(4,1)S(1)}, s32[]{:S(2)}) async-start(s8[8388608]{0:T(1024)(128)(4,1)} %bitcast.214), calls=%async_computation.8 | async-start | bytes 8388608
  281.0 26.5 %slice-start.3 = ((s8[8388608]{0:T(1024)(128)(4,1)}), s8[4194304]{0:T(1024)(128)(4,1)S(1)}, s32[]{:S(2)}) async-start(s8[8388608]{0:T(1024)(128)(4,1)} %bitcast.214), calls=%async_computation.9 | async-start | bytes 8388608
  351.2 22.7 %slice-start.8 = ((s8[8388608]{0:T(1024)(128)(4,1)}), s8[4194304]{0:T(1024)(128)(4,1)S(1)}, s32[]{:S(2)}) async-start(s8[8388608]{0:T(1024)(128)(4,1)} %bitcast.218), calls=%async_computation.14 | async-start | bytes 8388608
  355.9 17.9 %slice-start.9 = ((s8[8388608]{0:T(1024)(128)(4,1)}), s8[4194304]{0:T(1024)(128)(4,1)S(1)}, s32[]{:S(2)}) async-start(s8[8388608]{0:T(1024)(128)(4,1)} %bitcast.218), calls=%async_computation.15 | async-start | bytes 8388608
  355.9 17.9 %copy-start.37 = (bf16[512,8,128]{2,0,1:T(8,128)(2,1)S(1)}, bf16[512,8,128]{2,0,1:T(8,128)(2,1)}, u32[]{:S(2)}) copy-start(bf16[512,8,128]{2,0,1:T(8,128)(2,1)} %copy.156) | copy-start | bytes 3145732
  356.0 17.9 %copy-start.39 = (f32[512,4,128]{2,0,1:T(8,128)S(1)}, f32[512,4,128]{2,0,1:T(8,128)}, u32[]{:S(2)}) copy-start(f32[512,4,128]{2,0,1:T(8,128)} %fusion.104) | copy-start | bytes 3145732
  424.7 198.9 %reduce-scatter.5.cloned.1.call-start = ((), (), s32[]{:S(2)}) async-start(), calls=%async_computation.5 | async-start | bytes 10027008 | tf_op jit(solution)/shard_map/reduce_scatter | solution.py:270
  461.5 26.1 %collective-permute-start.7 = (bf16[512,1024]{1,0:T(8,128)(2,1)S(1)}, bf16[512,1024]{1,0:T(8,128)(2,1)S(1)}, u32[]{:S(2)}, u32[]{:S(2)}) collective-permute-start(bf16[512,1024]{1,0:T(8,128)(2,1)S(1)} %fusion.87), channel_id=1, source_target_pairs={{0,1},{1,0},{2,3},{3,2},{4,5},{5,4},{6,7},{7,6},{8,9},{9,8},{10,11... | collective-permute-start | bytes 3145736 | tf_op jit(solution)/shard_map/ppermute | solution.py:170
  463.0 24.5 %slice-start.15 = ((s8[6291456]{0:T(1024)(128)(4,1)}), s8[4194304]{0:T(1024)(128)(4,1)S(1)}, s32[]{:S(2)}) async-start(s8[6291456]{0:T(1024)(128)(4,1)} %bitcast.253), calls=%async_computation.21 | async-start | bytes 8388608
  464.3 23.2 %copy-start.55 = (bf16[512,2048]{1,0:T(8,128)(2,1)S(1)}, bf16[512,2048]{1,0:T(8,128)(2,1)}, u32[]{:S(2)}) copy-start(bf16[512,2048]{1,0:T(8,128)(2,1)} %copy-done.54) | copy-start | bytes 6291460
  464.3 23.2 %slice-start.16 = ((s8[6291456]{0:T(1024)(128)(4,1)}), s8[2097152]{0:T(1024)(128)(4,1)S(1)}, s32[]{:S(2)}) async-start(s8[6291456]{0:T(1024)(128)(4,1)} %bitcast.253), calls=%async_computation.22 | async-start | bytes 4194304
  466.1 44.4 %collective-permute-start.3 = (bf16[512,1024]{1,0:T(8,128)(2,1)S(1)}, bf16[512,1024]{1,0:T(8,128)(2,1)S(1)}, u32[]{:S(2)}, u32[]{:S(2)}) collective-permute-start(bf16[512,1024]{1,0:T(8,128)(2,1)S(1)} %fusion.81), channel_id=1, source_target_pairs={{0,1},{1,0},{2,3},{3,2},{4,5},{5,4},{6,7},{7,6},{8,9},{9,8},{10,11... | collective-permute-start | bytes 3145736 | tf_op jit(solution)/shard_map/ppermute | solution.py:170
  467.7 22.6 %copy-start.64 = (f32[1024]{0:T(1024)S(1)}, f32[1024]{0:T(1024)}, u32[]{:S(2)}) copy-start(f32[1024]{0:T(1024)} %get-tuple-element.79) | copy-start | bytes 12292
  467.7 42.8 %copy-start.11 = (f32[512,1024]{1,0:T(8,128)S(1)}, f32[512,1024]{1,0:T(8,128)}, u32[]{:S(2)}) copy-start(f32[512,1024]{1,0:T(8,128)} %copy-done.10) | copy-start | bytes 6291460
  490.3 17.1 %collective-permute-start.8 = (f32[18,128]{1,0:T(8,128)S(1)}, f32[18,128]{1,0:T(8,128)S(1)}, u32[]{:S(2)}, u32[]{:S(2)}) collective-permute-start(f32[18,128]{1,0:T(8,128)S(1)} %maximum_bitcast_fusion.3), channel_id=1, source_target_pairs={{0,1},{1,0},{2,3},{3,2},{4,5},{5,4},{6,7},{7,6},{8,9},{9,8},{10,11... | collective-permute-start | bytes 27656 | tf_op jit(solution)/shard_map/ppermute | solution.py:139
  507.5 1.2 collective-permute-start.9
  508.6 10.1 %copy-start.25 = (bf16[512,1024]{1,0:T(8,128)(2,1)S(1)}, bf16[512,1024]{1,0:T(8,128)(2,1)}, u32[]{:S(2)}) copy-start(bf16[512,1024]{1,0:T(8,128)(2,1)} %param.39) | copy-start | bytes 3145732
  508.7 4.6 collective-permute-start.10
  513.3 3.7 collective-permute-start.11
  517.0 4.6 collective-permute-start.12
  (75 other events, 327.3 us)
Sparse Core Ops, SparseCore 0:
  10.9 64.1 all-gather.2
  77.3 79.5 all-gather.4
  424.8 84.4 reduce-scatter.2
  513.3 110.3 reduce-scatter.4
where the time goes:
time: 643 us; the launch traced here: 634 us
  waiting for transfers between devices  274 us (43%)
  matrix products  152 us (24%)
  other arithmetic  101 us (16%)
  local copies, waits for them, and re-layouts  70.6 us (11%)
  starting transfers between devices  19.5 us (3%)
  between operations  15.5 us (2%)
    reduce_scatter x1, waiting for transfers between devices, local(): lax.psum_scatter(grad_mlp_w, 'dp', scatter_dimension=0, tiled=True)  97.4 us
    ppermute x4, waiting for transfers between devices, scatter_rows(): got = lax.ppermute(sent, 'tensor', swap)  64.9 us
    ppermute x4, waiting for transfers between devices, gather_rows(): return jnp.concatenate((own, lax.ppermute(own, 'tensor', swap)), 0)  56.4 us
    dot_general x7, matrix products, matmul(): return jnp.dot(left, right, preferred_element_type=F32)  40.6 us
    all_gather x1, waiting for transfers between devices, local(): full_attn = lax.all_gather(shard_attn, 'dp', axis=0, tiled=True)  36.1 us
    dot_general x8, matrix products, contract_cols(): lax.dot_general(left, right, (((1,), (1,)), ((), ())), preferred_element_...  29.2 us
    dot_general x5, matrix products, contract_rows(): lax.dot_general(left, right, (((0,), (0,)), ((), ())), preferred_element_...  28.4 us
    unnamed x213, local copies, waits for them, and re-layouts  23.4 us
  transfers between devices with their start and end apart: 17, of which 13 were waited for; matrix products, arithmetic and copies ran while one was open for 26% of the time, Pallas kernels for 0%

commit v1 on v0

--- a/solution.py
+++ b/solution.py
@@ -203,7 +203,15 @@
             (query_proj, key_proj, value_proj, out_proj.reshape(shard_rows, -1)), 1
         )
         shard_mlp = jnp.concatenate((gate_proj, up_proj, down_proj.reshape(shard_rows, -1)), 1)
-        full_attn = lax.all_gather(shard_attn, "dp", axis=0, tiled=True)
+        ways, here, hop = (lax.axis_size("dp"), lax.axis_index("dp"), shard_attn.shape[0])
+        line, have = (shard_attn, 1)
+        while have < ways:
+            line = jnp.concatenate(
+                [line, lax.ppermute(line, "dp", [(d, (d - have) % ways) for d in range(ways)])],
+                axis=0,
+            )
+            have = 2 * have
+        full_attn = jnp.roll(line, here * hop, axis=0)
         full_mlp = lax.all_gather(shard_mlp, "dp", axis=0, tiled=True)
         proj_qkv = full_attn[:, :width_qkv]
         full_out = full_attn[:, width_qkv:].reshape(-1, width)

time: 643 us -> 858 us (1.33)
  waiting for transfers between devices: 274 us -> 457 us
  local copies, waits for them, and re-layouts: 70.6 us -> 89.7 us
    ppermute x0 -> x4, waiting for transfers between devices: none -> 225 us  [local(): lax.ppermute(line, 'dp', [(d, (d - have) % ways) for d in range(ways)])]
    all_gather x1 -> x0, waiting for transfers between devices: 36.1 us -> none  [local(): full_attn = lax.all_gather(shard_attn, 'dp', axis=0, tiled=True)]
    unnamed x213 -> x217, local copies, waits for them, and re-layouts: 23.4 us -> 37.4 us
  transfers between devices with their start and end apart: 17 -> 20, of which waited for: 13 -> 16; matrix products, arithmetic and copies ran while one was open for 26% -> 22% of each run, Pallas kernels for 0% -> 0%
where the time goes in v1:
time: 858 us; the launch traced here: 847 us
  waiting for transfers between devices  457 us (53%)
  matrix products  157 us (18%)
  other arithmetic  105 us (12%)
  local copies, waits for them, and re-layouts  89.7 us (10%)
  starting transfers between devices  23.4 us (3%)
  between operations  15.4 us (2%)
    ppermute x4, waiting for transfers between devices, local(): lax.ppermute(line, 'dp', [(d, (d - have) % ways) for d in range(ways)])  225 us
    reduce_scatter x1, waiting for transfers between devices, local(): lax.psum_scatter(grad_mlp_w, 'dp', scatter_dimension=0, tiled=True)  97.8 us
    ppermute x4, waiting for transfers between devices, scatter_rows(): got = lax.ppermute(sent, 'tensor', swap)  63.9 us
    ppermute x4, waiting for transfers between devices, gather_rows(): return jnp.concatenate((own, lax.ppermute(own, 'tensor', swap)), 0)  51.7 us
    dot_general x7, matrix products, matmul(): return jnp.dot(left, right, preferred_element_type=F32)  41.5 us
    unnamed x217, local copies, waits for them, and re-layouts  37.4 us
    dot_general x8, matrix products, contract_cols(): lax.dot_general(left, right, (((1,), (1,)), ((), ())), preferred_element_...  31.3 us
    dot_general x5, matrix products, contract_rows(): lax.dot_general(left, right, (((0,), (0,)), ((), ())), preferred_element_...  30.1 us
  transfers between devices with their start and end apart: 20, of which 16 were waited for; matrix products, arithmetic and copies ran while one was open for 22% of the time, Pallas kernels for 0%

profile of v1, /device:TPU:0, one launch (start us, length us, event | category | flops | bytes accessed | tf_op | source)
XLA Modules:
  0.0 847.2 jit_solution(1728065280918379921)
XLA Ops:
  13.4 5.4 collective-permute-start.1
  18.8 5.3 collective-permute-done.1
  24.8 17.3 %collective-permute-done.2 = bf16[128,3072]{1,0:T(8,128)(2,1)S(1)} collective-permute-done((bf16[128,3072]{1,0:T(8,128)(2,1)S(1)}, bf16[128,3072]{1,0:T(8,128)(2,1)S(1)}, u32[]{:S(2)}, u32[]{:S(2)}) %collective-permute-start.2) | collective-permute-done | bytes 786464 | tf_op jit(solution)/shard_map/ppermute | solution.py:210
  42.8 36.5 %collective-permute-done.3 = bf16[256,3072]{1,0:T(8,128)(2,1)S(1)} collective-permute-done((bf16[256,3072]{1,0:T(8,128)(2,1)S(1)}, bf16[256,3072]{1,0:T(8,128)(2,1)S(1)}, u32[]{:S(2)}, u32[]{:S(2)}) %collective-permute-start.3) | collective-permute-done | bytes 1572896 | tf_op jit(solution)/shard_map/ppermute | solution.py:210
  87.5 3.1 fusion.119
  92.6 14.3 %collective-permute-done = bf16[512,1024]{1,0:T(8,128)(2,1)} collective-permute-done((bf16[512,1024]{1,0:T(8,128)(2,1)}, bf16[512,1024]{1,0:T(8,128)(2,1)}, u32[]{:S(2)}, u32[]{:S(2)}) %collective-permute-start) | collective-permute-done | bytes 1048608 | tf_op jit(solution)/shard_map/ppermute | solution.py:150
  111.1 165.5 %collective-permute-done.4 = bf16[512,3072]{1,0:T(8,128)(2,1)} collective-permute-done((bf16[512,3072]{1,0:T(8,128)(2,1)}, bf16[512,3072]{1,0:T(8,128)(2,1)}, u32[]{:S(2)}, u32[]{:S(2)}) %collective-permute-start.4) | collective-permute-done | bytes 3145760 | tf_op jit(solution)/shard_map/ppermute | solution.py:210
  276.7 3.7 constant_dynamic-update-slice_fusion.9
  286.1 3.8 constant_dynamic-update-slice_fusion.4
  289.9 10.7 %fusion.36 = f32[1024,2048]{1,0:T(8,128)} fusion(bf16[2048,3072]{1,0:T(8,128)(2,1)} %constant_dynamic-update-slice_fusion.4, s32[]{:T(128)S(6)} %select_n.76, f32[1024]{0:T(1024)S(1)} %copy-done.71, f32[1024]{0:T(1024)S(1)} %add_rsqrt_fusion.2, bf16[512,1024]{1,0:T(8,128)(2,1)} %collective-permute-done, bf16[512,1024]{1,0:T(8,128)(2,1)} %param.26), kind=kOutput, calls=%fused_computation.77 | convolution fusion | flops 4302307328 | bytes 14688260 | tf_op jit(solution)/shard_map/dot_general | solution.py:48
  300.6 4.3 slice_select_fusion.1
  340.5 7.5 fusion.140
  348.0 8.2 fusion.3
  356.2 7.8 fusion.82
  366.2 3.6 fusion.86
  371.9 24.0 %collective-permute-done.5 = bf16[512,1024]{1,0:T(8,128)(2,1)S(1)} collective-permute-done((bf16[512,1024]{1,0:T(8,128)(2,1)S(1)}, bf16[512,1024]{1,0:T(8,128)(2,1)S(1)}, u32[]{:S(2)}, u32[]{:S(2)}) %collective-permute-start.5) | collective-permute-done | bytes 1048608 | tf_op jit(solution)/shard_map/ppermute | solution.py:170
  395.9 3.4 multiply_reduce_fusion.7
  403.4 15.0 %collective-permute-done.8 = bf16[512,1024]{1,0:T(8,128)(2,1)S(1)} collective-permute-done((bf16[512,1024]{1,0:T(8,128)(2,1)S(1)}, bf16[512,1024]{1,0:T(8,128)(2,1)S(1)}, u32[]{:S(2)}, u32[]{:S(2)}) %collective-permute-start.8) | collective-permute-done | bytes 1048608 | tf_op jit(solution)/shard_map/ppermute | solution.py:150
  419.5 3.8 slice.343
  423.3 5.9 reshape.389
  429.2 8.7 %fusion.141 = f32[1024,1536]{1,0:T(8,128)} fusion(bf16[1024,1024]{1,0:T(8,128)(2,1)} %constant_dynamic-update-slice_fusion.17, bf16[1536,1024]{1,0:T(8,128)(2,1)} %reshape.389), kind=kOutput, calls=%fused_computation.252 | convolution fusion | flops 3221225472 | bytes 11534336 | tf_op jit(solution)/shard_map/dot_general | solution.py:56
  440.0 8.5 %fusion.42 = f32[1024,1536]{1,0:T(8,128)} fusion(bf16[1024,4608]{1,0:T(8,128)(2,1)} %all-gather.2.cloned.1.call-done, bf16[512,1024]{1,0:T(8,128)(2,1)} %collective-permute-done.6, bf16[512,1024]{1,0:T(8,128)(2,1)} %multiply_convert_fusion.4), kind=kOutput, calls=%fused_computation.84 | convolution fusion | flops 3225419776 | bytes 11534336 | tf_op jit(solution)/shard_map/dot_general | solution.py:48
  448.6 10.6 %multiply_convert_fusion.1 = (bf16[1024,1536]{1,0:T(8,128)(2,1)S(1)}, bf16[1024,1536]{1,0:T(8,128)(2,1)}, bf16[1024,1536]{1,0:T(8,128)(2,1)S(1)}) fusion(f32[1024,1536]{1,0:T(8,128)} %fusion.141, f32[1024,1536]{1,0:T(8,128)} %fusion.42, bf16[1024,4608]{1,0:T(8,128)(2,1)S(1)} %bitcast.242, bf16[512,1024]{1,0:T(8,128)(2,1)} %collective-permute-done.6, ...), kind=kOutput, calls=%fused_computation.34 | convolution fusion | flops 3250585600 | bytes 27262976 | tf_op jit(solution)/shard_map/dot_general | solution.py:48
  466.3 20.8 %collective-permute-done.9 = bf16[512,1024]{1,0:T(8,128)(2,1)S(1)} collective-permute-done((bf16[512,1024]{1,0:T(8,128)(2,1)S(1)}, bf16[512,1024]{1,0:T(8,128)(2,1)S(1)}, u32[]{:S(2)}, u32[]{:S(2)}) %collective-permute-start.9) | collective-permute-done | bytes 1048608 | tf_op jit(solution)/shard_map/ppermute | solution.py:170
  494.9 20.3 %collective-permute-done.10 = bf16[512,1024]{1,0:T(8,128)(2,1)S(1)} collective-permute-done((bf16[512,1024]{1,0:T(8,128)(2,1)}, bf16[512,1024]{1,0:T(8,128)(2,1)S(1)}, u32[]{:S(2)}, u32[]{:S(2)}) %collective-permute-start.10) | collective-permute-done | bytes 1048608 | tf_op jit(solution)/shard_map/ppermute | solution.py:150
  515.2 4.7 convolution_convert_fusion.3
  523.0 2.9 fusion.10
  533.0 11.2 %fusion = (f32[4,2,512]{2,1,0:T(2,128)}, f32[4,1024,512,2]{2,1,3,0:T(8,128)}) fusion(f32[4,2,512,1024]{2,3,1,0:T(8,128)S(1)} %bitcast.217, f32[4,2,512]{2,1,0:T(2,128)} %bitcast.246, bf16[512,4,2,128]{0,3,2,1:T(8,128)(2,1)} %bitcast.230, bf16[1024,4,128,1]{2,1,0,3:T(4,128)(2,1)} %bitcast.236), kind=kOutput, calls=%fused_computation.2 | convolution fusion | flops 1086320640 | bytes 35684352 | tf_op jit(solution)/shard_map/qgrd,kgd->grqk/dot_general | solution.py:113
  544.3 8.4 fusion.2
  558.3 3.9 copy.226
  565.0 4.1 multiply_subtract_fusion
  569.7 16.9 %multiply_reduce_fusion = (f32[1024,8]{1,0:T(8,128)S(1)}, f32[1024,8,128]{2,1,0:T(8,128)}) fusion(f32[1024,8,128]{2,1,0:T(8,128)S(1)} %bitcast.221, f32[128]{0:T(128)S(1)} %copy-done.68, f32[1024,8]{1,0:T(8,128)S(1)} %copy-done.26, f32[1024,8,64]{2,1,0:T(8,128)S(1)} %get-tuple-element.89, f32[1024,8,64]{2,1,0:T(8,128)S(1)} %get-tuple-element.88), kind=kLoop, calls=%fused_computation.57 | loop fusion | flops 5234688 | bytes 12648960 | tf_op jit(solution)/shard_map/reduce_sum | solution.py:43
  595.3 10.0 %fusion.59 = bf16[1024,4,128]{0,2,1:T(8,128)(2,1)} fusion(f32[512,4,128]{0,2,1:T(8,128)} %fusion.102, bf16[512,4,2,128]{0,3,2,1:T(8,128)(2,1)S(1)} %bitcast.231, f32[4,2,512,1024]{2,3,1,0:T(8,128)} %get-tuple-element.137, f32[4,2,512]{2,1,0:T(2,128)S(1)} %bitcast.248), kind=kOutput, calls=%fused_computation.113 | convolution fusion | flops 1083179008 | bytes 19939328 | tf_op jit(solution)/shard_map/grqk,qgrd->kgd/dot_general | solution.py:127
  611.3 7.1 fusion.22
  624.5 4.4 fusion.60
  629.0 6.8 fusion.29
  635.8 3.2 pad_maximum_fusion.2
  640.8 6.9 convolution_convert_fusion
  647.8 4.6 reshape.393
  652.4 6.5 convolution_convert_fusion.2
  658.9 5.4 convolution_convert_fusion.1
  664.3 5.2 pad_maximum_fusion.1
  671.1 4.5 fusion.89
  682.7 19.1 %collective-permute-done.11 = bf16[512,1024]{1,0:T(8,128)(2,1)S(1)} collective-permute-done((bf16[512,1024]{1,0:T(8,128)(2,1)S(1)}, bf16[512,1024]{1,0:T(8,128)(2,1)S(1)}, u32[]{:S(2)}, u32[]{:S(2)}) %collective-permute-start.11) | collective-permute-done | bytes 1048608 | tf_op jit(solution)/shard_map/ppermute | solution.py:170
  701.8 5.1 multiply_reduce_fusion.3
  708.6 12.7 %collective-permute-done.12 = f32[18,128]{1,0:T(8,128)S(1)} collective-permute-done((f32[18,128]{1,0:T(8,128)S(1)}, f32[18,128]{1,0:T(8,128)S(1)}, u32[]{:S(2)}, u32[]{:S(2)}) %collective-permute-start.12) | collective-permute-done | bytes 9248 | tf_op jit(solution)/shard_map/ppermute | solution.py:139
  726.8 3.7 collective-permute-done.15
  739.7 97.8 %reduce-scatter.5.cloned.1.call-done = bf16[64,4608]{1,0:T(8,128)(2,1)} async-done(((bf16[1024,4608]{1,0:T(8,128)(2,1)}), bf16[64,4608]{1,0:T(8,128)(2,1)}) %reduce-scatter.5.cloned.1.call-update) | async-done | bytes 589840 | tf_op jit(solution)/shard_map/reduce_scatter | solution.py:278
  (341 shorter events, 158.6 us)
Async XLA Ops:
  7.2 412.3 %all-gather.2.cloned.1.call-start = ((), (), s32[]{:S(2)}) async-start(), calls=%async_computation.2 | async-start | bytes 10027008 | tf_op jit(solution)/shard_map/all_gather | solution.py:215
  13.4 10.7 %collective-permute-start.1 = (bf16[64,3072]{1,0:T(8,128)(2,1)S(1)}, bf16[64,3072]{1,0:T(8,128)(2,1)S(1)}, u32[]{:S(2)}, u32[]{:S(2)}) collective-permute-start(bf16[64,3072]{1,0:T(8,128)(2,1)S(1)} %get-tuple-element.119), channel_id=1, source_target_pairs={{0,30},{2,0},{4,2},{6,4},{8,6},{10,8},{12,10},{14,12},{16,14},{18,... | collective-permute-start | bytes 1179656 | tf_op jit(solution)/shard_map/ppermute | solution.py:210
  24.2 60.6 %copy-start.58 = (bf16[64,1536]{1,0:T(8,128)(2,1)S(1)}, bf16[64,1536]{1,0:T(8,128)(2,1)}, u32[]{:S(2)}) copy-start(bf16[64,1536]{1,0:T(8,128)(2,1)} %param.37) | copy-start | bytes 589828
  24.2 17.9 %collective-permute-start.2 = (bf16[128,3072]{1,0:T(8,128)(2,1)S(1)}, bf16[128,3072]{1,0:T(8,128)(2,1)S(1)}, u32[]{:S(2)}, u32[]{:S(2)}) collective-permute-start(bf16[128,3072]{1,0:T(8,128)(2,1)S(1)} %pad_maximum_fusion.15), channel_id=1, source_target_pairs={{0,28},{2,30},{4,0},{6,2},{8,4},{10,6},{12,8},{14,10},{16,12},{18,... | collective-permute-start | bytes 2359304 | tf_op jit(solution)/shard_map/ppermute | solution.py:210
  42.2 44.5 %copy-start.73 = (s32[1024]{0:T(1024)S(1)}, s32[1024]{0:T(1024)}, u32[]{:S(2)}) copy-start(s32[1024]{0:T(1024)} %param.27) | copy-start | bytes 12292
  42.2 37.1 %collective-permute-start.3 = (bf16[256,3072]{1,0:T(8,128)(2,1)S(1)}, bf16[256,3072]{1,0:T(8,128)(2,1)S(1)}, u32[]{:S(2)}, u32[]{:S(2)}) collective-permute-start(bf16[256,3072]{1,0:T(8,128)(2,1)S(1)} %pad_maximum_fusion.11), channel_id=1, source_target_pairs={{0,24},{2,26},{4,28},{6,30},{8,0},{10,2},{12,4},{14,6},{16,8},{18,... | collective-permute-start | bytes 4718600 | tf_op jit(solution)/shard_map/ppermute | solution.py:210
  81.1 195.5 %collective-permute-start.4 = (bf16[512,3072]{1,0:T(8,128)(2,1)}, bf16[512,3072]{1,0:T(8,128)(2,1)}, u32[]{:S(2)}, u32[]{:S(2)}) collective-permute-start(bf16[512,3072]{1,0:T(8,128)(2,1)} %pad_maximum_fusion.6), channel_id=1, source_target_pairs={{0,16},{2,18},{4,20},{6,22},{8,24},{10,26},{12,28},{14,30},{16,0},... | collective-permute-start | bytes 9437192 | tf_op jit(solution)/shard_map/ppermute | solution.py:210
  82.2 24.7 %collective-permute-start = (bf16[512,1024]{1,0:T(8,128)(2,1)}, bf16[512,1024]{1,0:T(8,128)(2,1)}, u32[]{:S(2)}, u32[]{:S(2)}) collective-permute-start(bf16[512,1024]{1,0:T(8,128)(2,1)} %param.26), channel_id=1, source_target_pairs={{0,1},{1,0},{2,3},{3,2},{4,5},{5,4},{6,7},{7,6},{8,9},{9,8},{10,11... | collective-permute-start | bytes 3145736 | tf_op jit(solution)/shard_map/ppermute | solution.py:150
  86.6 649.6 %reduce-scatter.3.cloned.1.call-start = ((), (), s32[]{:S(2)}) async-start(), calls=%async_computation.3 | async-start | bytes 6684672 | tf_op jit(solution)/shard_map/reduce_scatter | solution.py:315
  90.6 230.8 %copy-start.15 = (f32[1024,64]{1,0:T(8,128)}, f32[1024,64]{1,0:T(8,128)S(1)}, u32[]{:S(2)}) copy-start(f32[1024,64]{1,0:T(8,128)S(1)} %get-tuple-element.133) | copy-start | bytes 786436
  108.9 181.0 %copy-start.64 = (f32[1024]{0:T(1024)}, f32[1024]{0:T(1024)S(1)}, u32[]{:S(2)}) copy-start(f32[1024]{0:T(1024)S(1)} %add_rsqrt_fusion.2) | copy-start | bytes 12292
  109.8 170.5 %copy-start.50 = (bf16[64,1024]{1,0:T(8,128)(2,1)S(1)}, bf16[64,1024]{1,0:T(8,128)(2,1)}, u32[]{:S(2)}) copy-start(bf16[64,1024]{1,0:T(8,128)(2,1)} %param.32) | copy-start | bytes 393220
  109.9 171.2 %copy-start.56 = (bf16[64,512]{1,0:T(8,128)(2,1)S(1)}, bf16[64,512]{1,0:T(8,128)(2,1)}, u32[]{:S(2)}) copy-start(bf16[64,512]{1,0:T(8,128)(2,1)} %param.33) | copy-start | bytes 196612
  109.9 171.8 %copy-start.57 = (bf16[64,512]{1,0:T(8,128)(2,1)S(1)}, bf16[64,512]{1,0:T(8,128)(2,1)}, u32[]{:S(2)}) copy-start(bf16[64,512]{1,0:T(8,128)(2,1)} %param.34) | copy-start | bytes 196612
  109.9 172.5 %copy-start.51 = (bf16[64,1024]{1,0:T(8,128)(2,1)S(1)}, bf16[64,1024]{1,0:T(8,128)(2,1)}, u32[]{:S(2)}) copy-start(bf16[64,1024]{1,0:T(8,128)(2,1)} %param.35) | copy-start | bytes 393220
  309.0 23.3 %copy-start.8 = (f32[1024,512]{1,0:T(8,128)}, f32[1024,512]{1,0:T(8,128)S(1)}, u32[]{:S(2)}) copy-start(f32[1024,512]{1,0:T(8,128)S(1)} %fusion.50) | copy-start | bytes 6291460
  332.3 160.9 %copy-start.54 = (f32[1024,4]{0,1:T(4,128)}, f32[1024,4]{0,1:T(4,128)S(1)}, u32[]{:S(2)}) copy-start(f32[1024,4]{0,1:T(4,128)S(1)} %add_rsqrt_fusion.1) | copy-start | bytes 49156
  366.2 29.8 %copy-start.78 = (bf16[4,128,2,512]{3,1,2,0:T(8,128)(2,1)}, bf16[4,128,2,512]{3,1,2,0:T(8,128)(2,1)S(1)}, u32[]{:S(2)}) copy-start(bf16[4,128,2,512]{3,1,2,0:T(8,128)(2,1)S(1)} %get-tuple-element.111) | copy-start | bytes 3145732
  366.2 33.2 %copy-start.76 = (bf16[4,128,2,512]{3,1,2,0:T(8,128)(2,1)}, bf16[4,128,2,512]{3,1,2,0:T(8,128)(2,1)S(1)}, u32[]{:S(2)}) copy-start(bf16[4,128,2,512]{3,1,2,0:T(8,128)(2,1)S(1)} %get-tuple-element.110) | copy-start | bytes 3145732
  369.8 26.1 %collective-permute-start.5 = (bf16[512,1024]{1,0:T(8,128)(2,1)S(1)}, bf16[512,1024]{1,0:T(8,128)(2,1)S(1)}, u32[]{:S(2)}, u32[]{:S(2)}) collective-permute-start(bf16[512,1024]{1,0:T(8,128)(2,1)S(1)} %fusion.86), channel_id=1, source_target_pairs={{0,1},{1,0},{2,3},{3,2},{4,5},{5,4},{6,7},{7,6},{8,9},{9,8},{10,11... | collective-permute-start | bytes 3145736 | tf_op jit(solution)/shard_map/ppermute | solution.py:170
  371.4 47.0 %collective-permute-start.8 = (bf16[512,1024]{1,0:T(8,128)(2,1)S(1)}, bf16[512,1024]{1,0:T(8,128)(2,1)S(1)}, u32[]{:S(2)}, u32[]{:S(2)}) collective-permute-start(bf16[512,1024]{1,0:T(8,128)(2,1)S(1)} %copy-done.22), channel_id=1, source_target_pairs={{0,1},{1,0},{2,3},{3,2},{4,5},{5,4},{6,7},{7,6},{8,9},{9,8},{10,11... | collective-permute-start | bytes 3145736 | tf_op jit(solution)/shard_map/ppermute | solution.py:150
  399.4 90.6 %copy-start.10 = (f32[512,1024]{1,0:T(8,128)}, f32[512,1024]{1,0:T(8,128)S(1)}, u32[]{:S(2)}) copy-start(f32[512,1024]{1,0:T(8,128)S(1)} %get-tuple-element.139) | copy-start | bytes 6291460
  399.4 90.6 %copy-start.62 = (f32[512]{0:T(512)}, f32[512]{0:T(512)S(1)}, u32[]{:S(2)}) copy-start(f32[512]{0:T(512)S(1)} %add_rsqrt_fusion.3) | copy-start | bytes 6148
  400.9 39.2 %collective-permute-start.6 = (bf16[512,1024]{1,0:T(8,128)(2,1)}, bf16[512,1024]{1,0:T(8,128)(2,1)}, u32[]{:S(2)}, u32[]{:S(2)}) collective-permute-start(bf16[512,1024]{1,0:T(8,128)(2,1)} %multiply_convert_fusion.4), channel_id=1, source_target_pairs={{0,1},{1,0},{2,3},{3,2},{4,5},{5,4},{6,7},{7,6},{8,9},{9,8},{10,11... | collective-permute-start | bytes 3145736 | tf_op jit(solution)/shard_map/ppermute | solution.py:150
  429.2 19.4 %slice-start.10 = ((s8[9437184]{0:T(1024)(128)(4,1)}), s8[4194304]{0:T(1024)(128)(4,1)S(1)}, s32[]{:S(2)}) async-start(s8[9437184]{0:T(1024)(128)(4,1)} %bitcast.241), calls=%async_computation.15 | async-start | bytes 8388608
  429.2 19.4 %slice-start.11 = ((s8[9437184]{0:T(1024)(128)(4,1)}), s8[4194304]{0:T(1024)(128)(4,1)S(1)}, s32[]{:S(2)}) async-start(s8[9437184]{0:T(1024)(128)(4,1)} %bitcast.241), calls=%async_computation.16 | async-start | bytes 8388608
  459.2 28.0 %copy-start.80 = (bf16[1024,1536]{1,0:T(8,128)(2,1)}, bf16[1024,1536]{1,0:T(8,128)(2,1)S(1)}, u32[]{:S(2)}) copy-start(bf16[1024,1536]{1,0:T(8,128)(2,1)S(1)} %get-tuple-element.85) | copy-start | bytes 9437188
  462.9 24.3 %collective-permute-start.9 = (bf16[512,1024]{1,0:T(8,128)(2,1)S(1)}, bf16[512,1024]{1,0:T(8,128)(2,1)S(1)}, u32[]{:S(2)}, u32[]{:S(2)}) collective-permute-start(bf16[512,1024]{1,0:T(8,128)(2,1)S(1)} %add_convert_fusion.1), channel_id=1, source_target_pairs={{0,1},{1,0},{2,3},{3,2},{4,5},{5,4},{6,7},{7,6},{8,9},{9,8},{10,11... | collective-permute-start | bytes 3145736 | tf_op jit(solution)/shard_map/ppermute | solution.py:170
  466.3 23.7 %copy-start.23 = (bf16[512,1024]{1,0:T(8,128)(2,1)S(1)}, bf16[512,1024]{1,0:T(8,128)(2,1)}, u32[]{:S(2)}) copy-start(bf16[512,1024]{1,0:T(8,128)(2,1)} %param.39) | copy-start | bytes 3145732
  490.0 29.9 %copy-start.66 = (f32[512]{0:T(512)}, f32[512]{0:T(512)S(1)}, u32[]{:S(2)}) copy-start(f32[512]{0:T(512)S(1)} %broadcast_multiply_fusion.3) | copy-start | bytes 6148
  491.7 23.6 %collective-permute-start.10 = (bf16[512,1024]{1,0:T(8,128)(2,1)}, bf16[512,1024]{1,0:T(8,128)(2,1)S(1)}, u32[]{:S(2)}, u32[]{:S(2)}) collective-permute-start(bf16[512,1024]{1,0:T(8,128)(2,1)} %fusion.133), channel_id=1, source_target_pairs={{0,1},{1,0},{2,3},{3,2},{4,5},{5,4},{6,7},{7,6},{8,9},{9,8},{10,11... | collective-permute-start | bytes 3145736 | tf_op jit(solution)/shard_map/ppermute | solution.py:150
  494.3 26.8 %slice-start.2 = ((s8[8388608]{0:T(1024)(128)(4,1)}), s8[4194304]{0:T(1024)(128)(4,1)S(1)}, s32[]{:S(2)}) async-start(s8[8388608]{0:T(1024)(128)(4,1)} %bitcast.214), calls=%async_computation.7 | async-start | bytes 8388608
  494.9 26.2 %slice-start.3 = ((s8[8388608]{0:T(1024)(128)(4,1)}), s8[4194304]{0:T(1024)(128)(4,1)S(1)}, s32[]{:S(2)}) async-start(s8[8388608]{0:T(1024)(128)(4,1)} %bitcast.214), calls=%async_computation.8 | async-start | bytes 8388608
  565.0 22.5 %slice-start.8 = ((s8[8388608]{0:T(1024)(128)(4,1)}), s8[4194304]{0:T(1024)(128)(4,1)S(1)}, s32[]{:S(2)}) async-start(s8[8388608]{0:T(1024)(128)(4,1)} %bitcast.218), calls=%async_computation.13 | async-start | bytes 8388608
  569.7 17.7 %slice-start.9 = ((s8[8388608]{0:T(1024)(128)(4,1)}), s8[4194304]{0:T(1024)(128)(4,1)S(1)}, s32[]{:S(2)}) async-start(s8[8388608]{0:T(1024)(128)(4,1)} %bitcast.218), calls=%async_computation.14 | async-start | bytes 8388608
  569.7 17.7 %copy-start.35 = (bf16[512,8,128]{2,0,1:T(8,128)(2,1)S(1)}, bf16[512,8,128]{2,0,1:T(8,128)(2,1)}, u32[]{:S(2)}) copy-start(bf16[512,8,128]{2,0,1:T(8,128)(2,1)} %copy.156) | copy-start | bytes 3145732
  569.7 17.7 %copy-start.37 = (f32[512,4,128]{2,0,1:T(8,128)S(1)}, f32[512,4,128]{2,0,1:T(8,128)}, u32[]{:S(2)}) copy-start(f32[512,4,128]{2,0,1:T(8,128)} %fusion.106) | copy-start | bytes 3145732
  639.0 198.5 %reduce-scatter.5.cloned.1.call-start = ((), (), s32[]{:S(2)}) async-start(), calls=%async_computation.4 | async-start | bytes 10027008 | tf_op jit(solution)/shard_map/reduce_scatter | solution.py:278
  675.7 26.1 %collective-permute-start.11 = (bf16[512,1024]{1,0:T(8,128)(2,1)S(1)}, bf16[512,1024]{1,0:T(8,128)(2,1)S(1)}, u32[]{:S(2)}, u32[]{:S(2)}) collective-permute-start(bf16[512,1024]{1,0:T(8,128)(2,1)S(1)} %fusion.89), channel_id=1, source_target_pairs={{0,1},{1,0},{2,3},{3,2},{4,5},{5,4},{6,7},{7,6},{8,9},{9,8},{10,11... | collective-permute-start | bytes 3145736 | tf_op jit(solution)/shard_map/ppermute | solution.py:170
  679.5 22.3 %copy-start.47 = (bf16[512,2048]{1,0:T(8,128)(2,1)S(1)}, bf16[512,2048]{1,0:T(8,128)(2,1)}, u32[]{:S(2)}) copy-start(bf16[512,2048]{1,0:T(8,128)(2,1)} %copy-done.46) | copy-start | bytes 6291460
  681.3 42.7 %collective-permute-start.7 = (bf16[512,1024]{1,0:T(8,128)(2,1)S(1)}, bf16[512,1024]{1,0:T(8,128)(2,1)S(1)}, u32[]{:S(2)}, u32[]{:S(2)}) collective-permute-start(bf16[512,1024]{1,0:T(8,128)(2,1)S(1)} %fusion.83), channel_id=1, source_target_pairs={{0,1},{1,0},{2,3},{3,2},{4,5},{5,4},{6,7},{7,6},{8,9},{9,8},{10,11... | collective-permute-start | bytes 3145736 | tf_op jit(solution)/shard_map/ppermute | solution.py:170
  682.7 24.2 %copy-start.61 = (f32[1024]{0:T(1024)S(1)}, f32[1024]{0:T(1024)}, u32[]{:S(2)}) copy-start(f32[1024]{0:T(1024)} %get-tuple-element.79) | copy-start | bytes 12292
  682.7 41.3 %copy-start.11 = (f32[512,1024]{1,0:T(8,128)S(1)}, f32[512,1024]{1,0:T(8,128)}, u32[]{:S(2)}) copy-start(f32[512,1024]{1,0:T(8,128)} %copy-done.10) | copy-start | bytes 6291460
  706.9 14.4 %collective-permute-start.12 = (f32[18,128]{1,0:T(8,128)S(1)}, f32[18,128]{1,0:T(8,128)S(1)}, u32[]{:S(2)}, u32[]{:S(2)}) collective-permute-start(f32[18,128]{1,0:T(8,128)S(1)} %maximum_bitcast_fusion.3), channel_id=1, source_target_pairs={{0,1},{1,0},{2,3},{3,2},{4,5},{5,4},{6,7},{7,6},{8,9},{9,8},{10,11... | collective-permute-start | bytes 27656 | tf_op jit(solution)/shard_map/ppermute | solution.py:139
  721.3 1.2 collective-permute-start.13
  722.6 4.2 collective-permute-start.14
  726.8 3.7 collective-permute-start.15
  730.5 4.6 collective-permute-start.16
  (72 other events, 331.4 us)
Sparse Core Ops, SparseCore 0:
  86.7 160.1 all-gather.1
  639.1 83.8 reduce-scatter.2
  727.1 110.3 reduce-scatter.4
